TPU v7x, 256 devices: a whole 4x4x8 slice. The times are simulated.
256 devices in a mesh: seq: 16 (over y_hi, x, core), dp: 16 (over y_lo, z).
Axes of the slice: x: 4, y: 4 (y_hi: 2, y_lo: 2; y = y_hi * 2 + y_lo), z: 8, core: 2. Of those that a mesh axis runs over, the one named last changes fastest.
Arguments:
- query: bfloat16 [16, 3072, 1280], P('dp', 'seq'), may hold values from -52 to 52, as said below
- keys: bfloat16 [16, 3072, 1280], P('dp', 'seq'), may hold values from -6 to 6, as said below
- values: bfloat16 [16, 3072, 1280], P('dp', 'seq'), may hold values from -6 to 6
- attn: bfloat16 [16, 3072, 1280], P('dp', 'seq'), may hold values from -6 to 6
- d_block: bfloat16 [16, 3072, 1280], P('dp', 'seq'), may hold values from -6 to 6
- w_out: bfloat16 [1280, 1280], P('dp'), may hold values from -0.15625 to 0.15625
Outputs:
- d_query: bfloat16 [16, 3072, 1280], P('dp', 'seq')
- d_keys: bfloat16 [16, 3072, 1280], P('dp', 'seq')
- d_values: bfloat16 [16, 3072, 1280], P('dp', 'seq')
- d_weight: float32 [1280, 1280], P('dp')
Inputs may be any that keep to these rules, and one draw needn't show every extreme that they name: Some query patches may lie along the sum of two keys of the same video. keys has entries of order one.
All inputs are finite; a program needn't handle non-finite values.
Results may differ from a plain program's by a relative error of at most 0.0058.
Values may be sent and summed in bfloat16 or wider, within the bound.
No kernel may reach another device: no remote copies, remote signals or barrier semaphores. Data moves between devices by JAX's collectives and lax.ppermute only.
A program may use at most 64 MiB of HBM per device.

v0:
```python
import jax
import jax.numpy as jnp
from jax import lax
from jax.sharding import Mesh
from jax.sharding import PartitionSpec as P

HEAD_DIM = 80
DP = ("dp_0", "dp_1")


def reduced_to_own(blocks, axes, order):
    lengths = [lax.axis_size(a) for a in axes]
    blocks = blocks.reshape(*lengths, *blocks.shape[1:])
    blocks = blocks.transpose(*order, *range(len(axes), blocks.ndim))
    blocks = blocks.reshape(-1, *blocks.shape[len(axes) :])
    for k in order:
        blocks = lax.psum_scatter(blocks, axes[k], scatter_dimension=0, tiled=True)
    return blocks[0]


def split_up(x, dim, size):
    before, after = (x.shape[:dim], x.shape[dim + 1 :])
    return jnp.moveaxis(x.reshape(*before, size, -1, *after), dim, 0)


def scatter_axes(x, axes, order, dim):
    size = lax.axis_size(axes)
    return reduced_to_own(split_up(x, dim, size), axes, order)


def over_pieces(x, axis):
    blocks = lax.all_gather(x, axis)
    return blocks.sum(axis=0)


def head_backward(query_h, keys_h, values_h, dout_h, delta_h):
    patch_total = query_h.shape[0]
    block_rows = min(512, patch_total)
    while patch_total % block_rows != 0:
        block_rows = block_rows // 2
    block_total = patch_total // block_rows
    score_scale = HEAD_DIM ** (-0.5)
    contract_last = (((1,), (1,)), ((), ()))
    contract_first = (((0,), (0,)), ((), ()))

    def one_block(carry, inputs):
        keys_grad, values_grad = carry
        query_block, dout_block, delta_block = inputs
        scores = (
            lax.dot_general(query_block, keys_h, contract_last, preferred_element_type=jnp.float32)
            * score_scale
        )
        row_max = jnp.max(scores, axis=1, keepdims=True)
        lse = row_max + jnp.log(jnp.sum(jnp.exp(scores - row_max), axis=1, keepdims=True))
        probs = jnp.exp(scores - lse)
        probs_low = probs.astype(jnp.bfloat16)
        values_grad = values_grad + lax.dot_general(
            probs_low, dout_block, contract_first, preferred_element_type=jnp.float32
        )
        d_probs = lax.dot_general(
            dout_block, values_h, contract_last, preferred_element_type=jnp.float32
        )
        d_scores = (score_scale * probs * (d_probs - delta_block[:, None])).astype(jnp.bfloat16)
        query_grad = jnp.dot(d_scores, keys_h, preferred_element_type=jnp.float32)
        keys_grad = keys_grad + lax.dot_general(
            d_scores, query_block, contract_first, preferred_element_type=jnp.float32
        )
        return ((keys_grad, values_grad), query_grad.astype(jnp.bfloat16))

    empty = jnp.zeros((patch_total, HEAD_DIM), jnp.float32)
    blocked = (
        query_h.reshape(block_total, block_rows, HEAD_DIM),
        dout_h.reshape(block_total, block_rows, HEAD_DIM),
        delta_h.reshape(block_total, block_rows),
    )
    (keys_grad, values_grad), query_blocks = lax.scan(one_block, (empty, empty), blocked)
    return (
        query_blocks.reshape(patch_total, HEAD_DIM),
        keys_grad.astype(jnp.bfloat16),
        values_grad.astype(jnp.bfloat16),
    )


def body(query, keys, values, attn, d_block, w_out):
    seq_count = lax.axis_size("seq")
    dp_count = lax.axis_size(DP)
    tok_rows = query.shape[1]
    features = query.shape[2]
    head_here = features // HEAD_DIM // seq_count
    grad_y = d_block.reshape(tok_rows, features)
    attn_rows = attn.reshape(tok_rows, features)
    d_out = lax.dot_general(
        grad_y,
        lax.all_gather(w_out, DP, axis=0, tiled=True),
        (((1,), (1,)), ((), ())),
        preferred_element_type=jnp.float32,
    ).astype(jnp.bfloat16)

    def split_heads(array):
        return array.reshape(tok_rows, seq_count, head_here, HEAD_DIM)

    row_local = jnp.sum(
        split_heads(d_out).astype(jnp.float32) * split_heads(attn_rows).astype(jnp.float32), axis=3
    )
    row_terms = lax.all_to_all(row_local, "seq", split_axis=1, concat_axis=0, tiled=True)
    query_all, keys_all, values_all, dout_all = (
        lax.all_to_all(split_heads(query), "seq", split_axis=1, concat_axis=0, tiled=True),
        lax.all_to_all(split_heads(keys), "seq", split_axis=1, concat_axis=0, tiled=True),
        lax.all_to_all(split_heads(values), "seq", split_axis=1, concat_axis=0, tiled=True),
        lax.all_to_all(split_heads(d_out), "seq", split_axis=1, concat_axis=0, tiled=True),
    )
    gradient = head_backward(
        query_all[:, 0, 0],
        keys_all[:, 0, 0],
        values_all[:, 0, 0],
        dout_all[:, 0, 0],
        row_terms[:, 0, 0],
    )
    query_list = [gradient[0]]
    keys_list = [gradient[1]]
    values_list = [gradient[2]]
    query_heads = jnp.stack(query_list, axis=1)[:, None]
    keys_heads = jnp.stack(keys_list, axis=1)[:, None]
    values_heads = jnp.stack(values_list, axis=1)[:, None]
    query_back, keys_back, values_back = (
        lax.all_to_all(query_heads, "seq", split_axis=0, concat_axis=1, tiled=True),
        lax.all_to_all(keys_heads, "seq", split_axis=0, concat_axis=1, tiled=True),
        lax.all_to_all(values_heads, "seq", split_axis=0, concat_axis=1, tiled=True),
    )
    factor = 1.0 / float(dp_count * tok_rows * seq_count) ** 0.5
    contract_first = (((0,), (0,)), ((), ()))
    partial_rows = scatter_axes(
        lax.dot_general(attn_rows, grad_y, contract_first, preferred_element_type=jnp.float32)
        * factor,
        DP,
        (1, 0),
        0,
    )
    d_weight = over_pieces(partial_rows, "seq")
    shape_out = (1, tok_rows, features)
    return (
        query_back.reshape(shape_out),
        keys_back.reshape(shape_out),
        values_back.reshape(shape_out),
        d_weight,
    )


def solution(mesh):
    finer = Mesh(mesh.devices.reshape(mesh.shape["seq"], 2, 8), ("seq", "dp_0", "dp_1"))
    in_specs = (
        P(DP, "seq", None),
        P(DP, "seq", None),
        P(DP, "seq", None),
        P(DP, "seq", None),
        P(DP, "seq", None),
        P(DP, None),
    )
    out_specs = (P(DP, "seq", None), P(DP, "seq", None), P(DP, "seq", None), P(DP, None))
    return jax.shard_map(body, mesh=finer, in_specs=in_specs, out_specs=out_specs, check_vma=False)
```

profile of v0, /device:TPU:1, one launch (start us, length us, event | category | flops | bytes accessed | tf_op | source)
XLA Modules:
  0.0 369.2 jit_solution(4399982114246284704)
XLA Ops:
  9.0 2.1 convolution_multiply_fusion
  11.1 3.2 copy.106
  16.5 8.4 %all-to-all-start.3 = ((bf16[192,16,1,80]{0,3,2,1:T(8,128)(2,1)}), bf16[192,16,1,80]{0,3,2,1:T(8,128)(2,1)S(1)}, u32[]{:S(2)}, u32[]{:S(2)}) async-start(bf16[192,16,1,80]{0,3,2,1:T(8,128)(2,1)} %bitcast.17), calls=%async_computation.3 | async-start | bytes 1310720 | tf_op jit(solution)/shard_map/all_to_all | solution.py:109
  25.0 84.7 %reduce-scatter.3.cloned.1.call-done = f32[2,80,1280]{2,1,0:T(8,128)} async-done(((f32[16,80,1280]{2,1,0:T(8,128)}), f32[2,80,1280]{2,1,0:T(8,128)}) %reduce-scatter.3.cloned.1.call-update) | async-done | bytes 819216 | tf_op jit(solution)/shard_map/reduce_scatter | solution.py:17
  110.8 7.6 %all-to-all-start = ((bf16[192,16,1,80]{0,3,2,1:T(8,128)(2,1)}), bf16[192,16,1,80]{0,3,2,1:T(8,128)(2,1)S(1)}, u32[]{:S(2)}, u32[]{:S(2)}) async-start(bf16[192,16,1,80]{0,3,2,1:T(8,128)(2,1)} %bitcast.1), calls=%async_computation | async-start | bytes 1310720 | tf_op jit(solution)/shard_map/all_to_all | solution.py:107
  120.6 18.7 %all-to-all-done = bf16[192,16,1,80]{0,3,2,1:T(8,128)(2,1)S(1)} async-done(((bf16[192,16,1,80]{0,3,2,1:T(8,128)(2,1)}), bf16[192,16,1,80]{0,3,2,1:T(8,128)(2,1)S(1)}, u32[]{:S(2)}, u32[]{:S(2)}) %all-to-all-start) | async-done | bytes 491552 | tf_op jit(solution)/shard_map/all_to_all | solution.py:107
  139.3 4.8 %all-to-all-start.1 = ((bf16[192,16,1,80]{0,3,2,1:T(8,128)(2,1)}), bf16[192,16,1,80]{0,3,2,1:T(8,128)(2,1)S(1)}, u32[]{:S(2)}, u32[]{:S(2)}) async-start(bf16[192,16,1,80]{0,3,2,1:T(8,128)(2,1)} %bitcast.124), calls=%async_computation.1 | async-start | bytes 1310720 | tf_op jit(solution)/shard_map/all_to_all | solution.py:108
  144.1 3.2 convolution_convert_fusion.1
  149.9 7.1 %all-to-all-done.1 = bf16[192,16,1,80]{0,3,2,1:T(8,128)(2,1)S(1)} async-done(((bf16[192,16,1,80]{0,3,2,1:T(8,128)(2,1)}), bf16[192,16,1,80]{0,3,2,1:T(8,128)(2,1)S(1)}, u32[]{:S(2)}, u32[]{:S(2)}) %all-to-all-start.1) | async-done | bytes 491552 | tf_op jit(solution)/shard_map/all_to_all | solution.py:108
  157.0 11.4 %all_to_all.120 = f32[192,16,1]{0,2,1:T(1,128)S(1)} all-to-all(f32[192,16,1]{0,2,1:T(1,128)S(1)} %reduce_sum.30), channel_id=1, replica_groups=mesh['seq'=16,'dp_0'=2,'dp_1'=8] {'seq'}, dimensions={1} | all-to-all | bytes 24576 | tf_op jit(solution)/shard_map/all_to_all | solution.py:105
  168.4 4.4 %all-to-all-start.2 = ((bf16[192,16,1,80]{0,3,2,1:T(8,128)(2,1)}), bf16[192,16,1,80]{0,3,2,1:T(8,128)(2,1)}, u32[]{:S(2)}, u32[]{:S(2)}) async-start(bf16[192,16,1,80]{0,3,2,1:T(8,128)(2,1)} %bitcast.12), calls=%async_computation.2 | async-start | bytes 1310720 | tf_op jit(solution)/shard_map/all_to_all | solution.py:110
  174.3 2.3 copy.110
  178.3 7.7 %all-to-all-done.2 = bf16[192,16,1,80]{0,3,2,1:T(8,128)(2,1)} async-done(((bf16[192,16,1,80]{0,3,2,1:T(8,128)(2,1)}), bf16[192,16,1,80]{0,3,2,1:T(8,128)(2,1)}, u32[]{:S(2)}, u32[]{:S(2)}) %all-to-all-start.2) | async-done | bytes 491552 | tf_op jit(solution)/shard_map/all_to_all | solution.py:110
  186.0 2.3 copy.112
  188.3 101.8 %while.15 = (s32[]{:T(128)}, f32[3072,80]{0,1:T(8,128)S(1)}, f32[3072,80]{0,1:T(8,128)S(1)}, bf16[6,512,80]{1,2,0:T(8,128)(2,1)}, bf16[6,512,80]{2,1,0:T(8,128)(...) while((s32[]{:T(128)}, f32[3072,80]{0,1:T(8,128)S(1)}, ...), condition=%wide.region_4.5_spmd.clone, body=%wide.region_1.4_spmd.clone.sunk | while | flops 1281334784 | bytes 91267760 | solution.py:76
  188.3 2.0 multiply_reduce_fusion.2
  190.3 2.6 copy-done.2
  194.1 4.5 %convolution_add_fusion.5 = f32[3072,80]{0,1:T(8,128)S(1)} fusion(f32[512,3072]{1,0:T(8,128)} %copy-done.2, f32[512]{0:T(512)S(1)} %log_add_fusion.2, f32[3072,80]{0,1:T(8,128)S(1)} %get-tuple-element.223, pred[]{:T(512)S(6)} %compare.3, bf16[6,512,80]{2,1,0:T(8,128)(2,1)} %get-tuple-element.238, s32[]{:T(128)} %get-tuple-element.221), kind=kOutput, calls=%fused_computation.5.clone.1 | convolution fusion | flops 256868352 | bytes 8391169 | tf_op jit(solution)/shard_map/while/body/eval_jaxpr/dot_general | solution.py:57
  198.9 3.0 multiply_convert_fusion.2
  201.9 1.7 convolution_add_fusion.4
  203.7 1.7 fusion.49
  205.4 2.0 multiply_reduce_fusion.2
  207.4 2.6 copy-done.2
  211.1 4.3 %convolution_add_fusion.5 = f32[3072,80]{0,1:T(8,128)S(1)} fusion(f32[512,3072]{1,0:T(8,128)} %copy-done.2, f32[512]{0:T(512)S(1)} %log_add_fusion.2, f32[3072,80]{0,1:T(8,128)S(1)} %get-tuple-element.223, pred[]{:T(512)S(6)} %compare.3, bf16[6,512,80]{2,1,0:T(8,128)(2,1)} %get-tuple-element.238, s32[]{:T(128)} %get-tuple-element.221), kind=kOutput, calls=%fused_computation.5.clone.1 | convolution fusion | flops 256868352 | bytes 8391169 | tf_op jit(solution)/shard_map/while/body/eval_jaxpr/dot_general | solution.py:57
  215.8 3.0 multiply_convert_fusion.2
  218.8 1.7 convolution_add_fusion.4
  220.5 1.7 fusion.49
  222.2 2.0 multiply_reduce_fusion.2
  224.2 2.6 copy-done.2
  228.0 4.4 %convolution_add_fusion.5 = f32[3072,80]{0,1:T(8,128)S(1)} fusion(f32[512,3072]{1,0:T(8,128)} %copy-done.2, f32[512]{0:T(512)S(1)} %log_add_fusion.2, f32[3072,80]{0,1:T(8,128)S(1)} %get-tuple-element.223, pred[]{:T(512)S(6)} %compare.3, bf16[6,512,80]{2,1,0:T(8,128)(2,1)} %get-tuple-element.238, s32[]{:T(128)} %get-tuple-element.221), kind=kOutput, calls=%fused_computation.5.clone.1 | convolution fusion | flops 256868352 | bytes 8391169 | tf_op jit(solution)/shard_map/while/body/eval_jaxpr/dot_general | solution.py:57
  232.7 3.0 multiply_convert_fusion.2
  235.7 1.7 convolution_add_fusion.4
  237.5 1.7 fusion.49
  239.2 2.0 multiply_reduce_fusion.2
  241.2 2.6 copy-done.2
  244.9 4.4 %convolution_add_fusion.5 = f32[3072,80]{0,1:T(8,128)S(1)} fusion(f32[512,3072]{1,0:T(8,128)} %copy-done.2, f32[512]{0:T(512)S(1)} %log_add_fusion.2, f32[3072,80]{0,1:T(8,128)S(1)} %get-tuple-element.223, pred[]{:T(512)S(6)} %compare.3, bf16[6,512,80]{2,1,0:T(8,128)(2,1)} %get-tuple-element.238, s32[]{:T(128)} %get-tuple-element.221), kind=kOutput, calls=%fused_computation.5.clone.1 | convolution fusion | flops 256868352 | bytes 8391169 | tf_op jit(solution)/shard_map/while/body/eval_jaxpr/dot_general | solution.py:57
  249.9 3.0 multiply_convert_fusion.2
  252.9 1.7 convolution_add_fusion.4
  254.6 1.7 fusion.49
  256.4 2.0 multiply_reduce_fusion.2
  258.3 2.6 copy-done.2
  262.1 4.3 %convolution_add_fusion.5 = f32[3072,80]{0,1:T(8,128)S(1)} fusion(f32[512,3072]{1,0:T(8,128)} %copy-done.2, f32[512]{0:T(512)S(1)} %log_add_fusion.2, f32[3072,80]{0,1:T(8,128)S(1)} %get-tuple-element.223, pred[]{:T(512)S(6)} %compare.3, bf16[6,512,80]{2,1,0:T(8,128)(2,1)} %get-tuple-element.238, s32[]{:T(128)} %get-tuple-element.221), kind=kOutput, calls=%fused_computation.5.clone.1 | convolution fusion | flops 256868352 | bytes 8391169 | tf_op jit(solution)/shard_map/while/body/eval_jaxpr/dot_general | solution.py:57
  266.8 3.0 multiply_convert_fusion.2
  269.8 1.7 convolution_add_fusion.4
  271.5 1.7 fusion.49
  273.2 2.0 multiply_reduce_fusion.2
  275.2 2.6 copy-done.2
  279.0 4.3 %convolution_add_fusion.5 = f32[3072,80]{0,1:T(8,128)S(1)} fusion(f32[512,3072]{1,0:T(8,128)} %copy-done.2, f32[512]{0:T(512)S(1)} %log_add_fusion.2, f32[3072,80]{0,1:T(8,128)S(1)} %get-tuple-element.223, pred[]{:T(512)S(6)} %compare.3, bf16[6,512,80]{2,1,0:T(8,128)(2,1)} %get-tuple-element.238, s32[]{:T(128)} %get-tuple-element.221), kind=kOutput, calls=%fused_computation.5.clone.1 | convolution fusion | flops 256868352 | bytes 8391169 | tf_op jit(solution)/shard_map/while/body/eval_jaxpr/dot_general | solution.py:57
  283.6 3.0 multiply_convert_fusion.2
  286.6 1.7 convolution_add_fusion.4
  288.3 1.7 fusion.49
  292.0 2.2 reshape.106
  294.3 4.1 %all-to-all-start.7 = ((bf16[16,2,7680]{2,1,0:T(2,128)(2,1)}), bf16[16,2,7680]{2,1,0:T(2,128)(2,1)S(1)}, u32[]{:S(2)}, u32[]{:S(2)}) async-start(bf16[16,2,7680]{2,1,0:T(2,128)(2,1)} %reshape.106), calls=%async_computation.7 | async-start | bytes 983040 | tf_op jit(solution)/shard_map/all_to_all | solution.py:128
  299.7 2.2 reshape.104
  301.9 7.6 %all-to-all-done.7 = bf16[16,2,7680]{2,1,0:T(2,128)(2,1)S(1)} async-done(((bf16[16,2,7680]{2,1,0:T(2,128)(2,1)}), bf16[16,2,7680]{2,1,0:T(2,128)(2,1)S(1)}, u32[]{:S(2)}, u32[]{:S(2)}) %all-to-all-start.7) | async-done | bytes 491552 | tf_op jit(solution)/shard_map/all_to_all | solution.py:128
  309.5 4.4 %all-to-all-start.6 = ((bf16[16,2,7680]{2,1,0:T(2,128)(2,1)}), bf16[16,2,7680]{2,1,0:T(2,128)(2,1)S(1)}, u32[]{:S(2)}, u32[]{:S(2)}) async-start(bf16[16,2,7680]{2,1,0:T(2,128)(2,1)} %reshape.104), calls=%async_computation.6 | async-start | bytes 983040 | tf_op jit(solution)/shard_map/all_to_all | solution.py:127
  315.7 17.0 %reduce.3 = bf16[3072,80]{1,0:T(8,128)(2,1)S(1)} reduce(bf16[3072,1,1,80]{3,2,1,0:T(2,128)(2,1)S(1)} %reshape.100, bf16[]{:T(256)} %broadcast.25), dimensions={1,2}, to_apply=%reshape.100.reduce_sub_computation | reduce | bytes 983042 | tf_op jit(solution)/shard_map/broadcast_in_dim;stack;reshape | solution.py:122
  332.7 2.2 reshape.102
  334.9 7.3 %all-to-all-start.5 = ((bf16[16,2,7680]{2,1,0:T(2,128)(2,1)}), bf16[16,2,7680]{2,1,0:T(2,128)(2,1)S(1)}, u32[]{:S(2)}, u32[]{:S(2)}) async-start(bf16[16,2,7680]{2,1,0:T(2,128)(2,1)} %reshape.102), calls=%async_computation.5 | async-start | bytes 983040 | tf_op jit(solution)/shard_map/all_to_all | solution.py:126
  342.2 1.6 reshape.107
  343.8 1.6 copy.104
  347.3 1.6 reshape.105
  353.0 1.6 reshape.103
  358.1 4.0 %reduce_sum.31 = f32[80,1280]{1,0:T(8,128)} reduce(f32[16,80,1280]{2,1,0:T(8,128)} %all-gather.5.cloned.1.call-done, f32[]{:T(128)} %constant.13.clone.1), dimensions={0}, to_apply=%region_7.8 | reduce | flops 1536000 | bytes 6963204 | tf_op jit(solution)/shard_map/reduce_sum | solution.py:33
  (99 shorter events, 35.7 us)
Async XLA Ops:
  8.0 1.0 copy-start
  8.0 101.7 %reduce-scatter.3.cloned.1.call-start = ((), (), s32[]{:S(2)}) async-start(), calls=%async_computation.11 | async-start | bytes 7372800 | tf_op jit(solution)/shard_map/reduce_scatter | solution.py:17
  14.3 1.0 copy-start.7
  14.3 95.4 %copy-start.8 = (bf16[1,192,1280]{2,1,0:T(8,128)(2,1)S(1)}, bf16[1,192,1280]{2,1,0:T(8,128)(2,1)}, u32[]{:S(2)}) copy-start(bf16[1,192,1280]{2,1,0:T(8,128)(2,1)} %param.8) | copy-start | bytes 1474564
  14.3 104.1 %copy-start.4 = (bf16[1,192,1280]{2,1,0:T(8,128)(2,1)S(1)}, bf16[1,192,1280]{2,1,0:T(8,128)(2,1)}, u32[]{:S(2)}) copy-start(bf16[1,192,1280]{2,1,0:T(8,128)(2,1)} %param.11) | copy-start | bytes 1474564
  14.4 105.1 %copy-start.9 = (bf16[1,192,1280]{2,1,0:T(8,128)(2,1)S(1)}, bf16[1,192,1280]{2,1,0:T(8,128)(2,1)}, u32[]{:S(2)}) copy-start(bf16[1,192,1280]{2,1,0:T(8,128)(2,1)} %param.9) | copy-start | bytes 1474564
  14.4 129.7 %all-gather.3.cloned.1.call-start = ((), (), s32[]{:S(2)}) async-start(), calls=%async_computation.10 | async-start | bytes 3481600 | tf_op jit(solution)/shard_map/all_gather | solution.py:94
  16.5 94.4 %all-to-all-start.3 = ((bf16[192,16,1,80]{0,3,2,1:T(8,128)(2,1)}), bf16[192,16,1,80]{0,3,2,1:T(8,128)(2,1)S(1)}, u32[]{:S(2)}, u32[]{:S(2)}) async-start(bf16[192,16,1,80]{0,3,2,1:T(8,128)(2,1)} %bitcast.17), calls=%async_computation.3 | async-start | bytes 1310720 | tf_op jit(solution)/shard_map/all_to_all | solution.py:109
  24.9 163.4 %reduce-scatter.5.cloned.1.call-start = ((), (), s32[]{:S(2)}) async-start(), calls=%async_computation.12 | async-start | bytes 1228800 | tf_op jit(solution)/shard_map/reduce_scatter | solution.py:17
  110.8 28.5 %all-to-all-start = ((bf16[192,16,1,80]{0,3,2,1:T(8,128)(2,1)}), bf16[192,16,1,80]{0,3,2,1:T(8,128)(2,1)S(1)}, u32[]{:S(2)}, u32[]{:S(2)}) async-start(bf16[192,16,1,80]{0,3,2,1:T(8,128)(2,1)} %bitcast.1), calls=%async_computation | async-start | bytes 1310720 | tf_op jit(solution)/shard_map/all_to_all | solution.py:107
  139.3 33.5 %copy-start.5 = (bf16[192,16,1,80]{0,3,2,1:T(8,128)(2,1)}, bf16[192,16,1,80]{0,3,2,1:T(8,128)(2,1)S(1)}, u32[]{:S(2)}) copy-start(bf16[192,16,1,80]{0,3,2,1:T(8,128)(2,1)S(1)} %all-to-all-done) | copy-start | bytes 1474564
  139.3 17.7 %all-to-all-start.1 = ((bf16[192,16,1,80]{0,3,2,1:T(8,128)(2,1)}), bf16[192,16,1,80]{0,3,2,1:T(8,128)(2,1)S(1)}, u32[]{:S(2)}, u32[]{:S(2)}) async-start(bf16[192,16,1,80]{0,3,2,1:T(8,128)(2,1)} %bitcast.124), calls=%async_computation.1 | async-start | bytes 1310720 | tf_op jit(solution)/shard_map/all_to_all | solution.py:108
  157.0 16.1 %copy-start.6 = (bf16[192,16,1,80]{0,3,2,1:T(8,128)(2,1)}, bf16[192,16,1,80]{0,3,2,1:T(8,128)(2,1)S(1)}, u32[]{:S(2)}) copy-start(bf16[192,16,1,80]{0,3,2,1:T(8,128)(2,1)S(1)} %all-to-all-done.1) | copy-start | bytes 1474564
  168.4 17.6 %all-to-all-start.2 = ((bf16[192,16,1,80]{0,3,2,1:T(8,128)(2,1)}), bf16[192,16,1,80]{0,3,2,1:T(8,128)(2,1)}, u32[]{:S(2)}, u32[]{:S(2)}) async-start(bf16[192,16,1,80]{0,3,2,1:T(8,128)(2,1)} %bitcast.12), calls=%async_computation.2 | async-start | bytes 1310720 | tf_op jit(solution)/shard_map/all_to_all | solution.py:110
  172.8 185.3 %all-gather.5.cloned.1.call-start = ((), (), s32[]{:S(2)}) async-start(), calls=%async_computation.13 | async-start | bytes 6963200 | tf_op jit(solution)/shard_map/all_gather | solution.py:32
  190.3 2.6 copy-start.2
  194.1 4.9 %copy-start.3 = (f32[512,3072]{1,0:T(8,128)S(1)}, f32[512,3072]{1,0:T(8,128)}, u32[]{:S(2)}) copy-start(f32[512,3072]{1,0:T(8,128)} %copy-done.2) | copy-start | bytes 18874372 | tf_op jit(solution)/shard_map/while
  207.3 2.6 copy-start.2
  211.1 4.6 %copy-start.3 = (f32[512,3072]{1,0:T(8,128)S(1)}, f32[512,3072]{1,0:T(8,128)}, u32[]{:S(2)}) copy-start(f32[512,3072]{1,0:T(8,128)} %copy-done.2) | copy-start | bytes 18874372 | tf_op jit(solution)/shard_map/while
  224.2 2.6 copy-start.2
  228.0 4.7 %copy-start.3 = (f32[512,3072]{1,0:T(8,128)S(1)}, f32[512,3072]{1,0:T(8,128)}, u32[]{:S(2)}) copy-start(f32[512,3072]{1,0:T(8,128)} %copy-done.2) | copy-start | bytes 18874372 | tf_op jit(solution)/shard_map/while
  241.2 2.6 copy-start.2
  244.9 5.0 %copy-start.3 = (f32[512,3072]{1,0:T(8,128)S(1)}, f32[512,3072]{1,0:T(8,128)}, u32[]{:S(2)}) copy-start(f32[512,3072]{1,0:T(8,128)} %copy-done.2) | copy-start | bytes 18874372 | tf_op jit(solution)/shard_map/while
  258.3 2.6 copy-start.2
  262.1 4.6 %copy-start.3 = (f32[512,3072]{1,0:T(8,128)S(1)}, f32[512,3072]{1,0:T(8,128)}, u32[]{:S(2)}) copy-start(f32[512,3072]{1,0:T(8,128)} %copy-done.2) | copy-start | bytes 18874372 | tf_op jit(solution)/shard_map/while
  275.2 2.6 copy-start.2
  279.0 4.6 %copy-start.3 = (f32[512,3072]{1,0:T(8,128)S(1)}, f32[512,3072]{1,0:T(8,128)}, u32[]{:S(2)}) copy-start(f32[512,3072]{1,0:T(8,128)} %copy-done.2) | copy-start | bytes 18874372 | tf_op jit(solution)/shard_map/while
  294.3 15.2 %all-to-all-start.7 = ((bf16[16,2,7680]{2,1,0:T(2,128)(2,1)}), bf16[16,2,7680]{2,1,0:T(2,128)(2,1)S(1)}, u32[]{:S(2)}, u32[]{:S(2)}) async-start(bf16[16,2,7680]{2,1,0:T(2,128)(2,1)} %reshape.106), calls=%async_computation.7 | async-start | bytes 983040 | tf_op jit(solution)/shard_map/all_to_all | solution.py:128
  309.5 25.4 %all-to-all-start.6 = ((bf16[16,2,7680]{2,1,0:T(2,128)(2,1)}), bf16[16,2,7680]{2,1,0:T(2,128)(2,1)S(1)}, u32[]{:S(2)}, u32[]{:S(2)}) async-start(bf16[16,2,7680]{2,1,0:T(2,128)(2,1)} %reshape.104), calls=%async_computation.6 | async-start | bytes 983040 | tf_op jit(solution)/shard_map/all_to_all | solution.py:127
  334.9 18.1 %all-to-all-start.5 = ((bf16[16,2,7680]{2,1,0:T(2,128)(2,1)}), bf16[16,2,7680]{2,1,0:T(2,128)(2,1)S(1)}, u32[]{:S(2)}, u32[]{:S(2)}) async-start(bf16[16,2,7680]{2,1,0:T(2,128)(2,1)} %reshape.102), calls=%async_computation.5 | async-start | bytes 983040 | tf_op jit(solution)/shard_map/all_to_all | solution.py:126
  353.0 9.0 %copy-start.1 = (bf16[1,192,1280]{2,1,0:T(8,128)(2,1)S(1)}, bf16[1,192,1280]{2,1,0:T(8,128)(2,1)}, u32[]{:S(2)}) copy-start(bf16[1,192,1280]{2,1,0:T(8,128)(2,1)} %param.12) | copy-start | bytes 1474564
Sparse Core Ops, SparseCore 0:
  14.5 95.1 reduce-scatter.2
  112.2 40.2 reduce-scatter.4
  188.4 64.1 all-gather.4
Sparse Core Ops, SparseCore 1:
  16.6 123.8 all-gather.2
where the time goes:
time: 371 us; the launch traced here: 369 us
  waiting for transfers between devices  127 us (34%)
  matrix products  81.9 us (22%)
  local copies, waits for them, and re-layouts  60.2 us (16%)
  starting transfers between devices  41.3 us (11%)
  other arithmetic  31.5 us (8%)
  between operations  15.4 us (4%)
  blocking collectives  11.4 us (3%)
    reduce_scatter x2, waiting for transfers between devices, reduced_to_own(): blocks = lax.psum_scatter(blocks, axes[k], scatter_dimension=0, tiled=True)  84.7 us
    unnamed x35, local copies, waits for them, and re-layouts  28.3 us
    dot_general x6, matrix products, one_block(): lax.dot_general(probs_low, dout_block, contract_first, preferred_element_...  26.2 us
    all_to_all x1, waiting for transfers between devices, body(): lax.all_to_all(split_heads(query), 'seq', split_axis=1, concat_axis=0, ti...  18.7 us
    dot_general x6, matrix products, one_block(): lax.dot_general(dout_block, values_h, contract_last, preferred_element_ty...  17.9 us
    while x24, local copies, waits for them, and re-layouts  17.7 us
    another operation x1, other arithmetic, body(): query_heads = jnp.stack(query_list, axis=1)[:, None]  17 us
    dot_general x6, matrix products, one_block(): lax.dot_general(query_block, keys_h, contract_last, preferred_element_typ...  11.8 us
  transfers between devices with their start and end apart: 11, of which 6 were waited for; matrix products, arithmetic and copies ran while one was open for 39% of the time, Pallas kernels for 0%

commit v1 on v0

--- a/solution.py
+++ b/solution.py
@@ -123,7 +123,12 @@
     keys_heads = jnp.stack(keys_list, axis=1)[:, None]
     values_heads = jnp.stack(values_list, axis=1)[:, None]
     query_back, keys_back, values_back = (
-        lax.all_to_all(query_heads, "seq", split_axis=0, concat_axis=1, tiled=True),
+        jnp.concatenate(
+            lax.all_to_all(
+                jnp.stack(jnp.split(query_heads, lax.axis_size("seq"), axis=0)), "seq", 0, 0
+            ),
+            axis=1,
+        ),
         lax.all_to_all(keys_heads, "seq", split_axis=0, concat_axis=1, tiled=True),
         lax.all_to_all(values_heads, "seq", split_axis=0, concat_axis=1, tiled=True),
     )

time: 371 us -> 374 us (level)
  local copies, waits for them, and re-layouts: 60.2 us -> 74.8 us
  other arithmetic: 31.5 us -> 17.5 us
  waiting for transfers between devices: 127 us -> 134 us
    another operation x1 -> x0, other arithmetic: 17 us -> none  [body(): query_heads = jnp.stack(query_list, axis=1)[:, None]]
    unnamed x35 -> x48, local copies, waits for them, and re-layouts: 28.3 us -> 41.8 us
    all_to_all x1, waiting for transfers between devices: 0.01 us -> 6.55 us  [body(): lax.all_to_all(keys_heads, 'seq', split_axis=0, concat_axis=1, tiled=True)]
    all_to_all x1, waiting for transfers between devices: 0.59 us -> 6.88 us  [body(): lax.all_to_all(jnp.stack(jnp.split(query_heads, lax.axis_size('seq'), axi...]
    all_to_all x1, waiting for transfers between devices: 7.58 us -> 1.45 us  [body(): lax.all_to_all(values_heads, 'seq', split_axis=0, concat_axis=1, tiled=True)]
    while x24 -> x37, local copies, waits for them, and re-layouts: 17.7 us -> 20.8 us
  transfers between devices with their start and end apart: 11 -> 11, of which waited for: 6 -> 7; matrix products, arithmetic and copies ran while one was open for 39% -> 38% of each run, Pallas kernels for 0% -> 0%
where the time goes in v1:
time: 374 us; the launch traced here: 372 us
  waiting for transfers between devices  134 us (36%)
  matrix products  80 us (21%)
  local copies, waits for them, and re-layouts  74.8 us (20%)
  starting transfers between devices  39 us (10%)
  other arithmetic  17.5 us (5%)
  between operations  15.4 us (4%)
  blocking collectives  11.4 us (3%)
    reduce_scatter x2, waiting for transfers between devices, reduced_to_own(): blocks = lax.psum_scatter(blocks, axes[k], scatter_dimension=0, tiled=True)  84.7 us
    unnamed x48, local copies, waits for them, and re-layouts  41.8 us
    dot_general x6, matrix products, one_block(): lax.dot_general(probs_low, dout_block, contract_first, preferred_element_...  26.2 us
    all_to_all x1, waiting for transfers between devices, body(): lax.all_to_all(split_heads(query), 'seq', split_axis=1, concat_axis=0, ti...  18.7 us
    while x36, local copies, waits for them, and re-layouts  18.6 us
    dot_general x6, matrix products, one_block(): lax.dot_general(dout_block, values_h, contract_last, preferred_element_ty...  16.1 us
    dot_general x6, matrix products, one_block(): lax.dot_general(query_block, keys_h, contract_last, preferred_element_typ...  11.8 us
    all_to_all x1, blocking collectives, body(): lax.all_to_all(row_local, 'seq', split_axis=1, concat_axis=0, tiled=True)  11.4 us
  transfers between devices with their start and end apart: 11, of which 7 were waited for; matrix products, arithmetic and copies ran while one was open for 38% of the time, Pallas kernels for 0%

profile of v1, /device:TPU:1, one launch (start us, length us, event | category | flops | bytes accessed | tf_op | source)
XLA Modules:
  0.0 372.2 jit_solution(3194361169450053772)
XLA Ops:
  9.0 2.1 convolution_multiply_fusion
  11.1 3.2 copy.113
  16.4 8.4 %all-to-all-start.3 = ((bf16[192,16,1,80]{0,3,2,1:T(8,128)(2,1)}), bf16[192,16,1,80]{0,3,2,1:T(8,128)(2,1)S(1)}, u32[]{:S(2)}, u32[]{:S(2)}) async-start(bf16[192,16,1,80]{0,3,2,1:T(8,128)(2,1)} %bitcast.17), calls=%async_computation.3 | async-start | bytes 1310720 | tf_op jit(solution)/shard_map/all_to_all | solution.py:109
  24.9 84.7 %reduce-scatter.3.cloned.1.call-done = f32[2,80,1280]{2,1,0:T(8,128)} async-done(((f32[16,80,1280]{2,1,0:T(8,128)}), f32[2,80,1280]{2,1,0:T(8,128)}) %reduce-scatter.3.cloned.1.call-update) | async-done | bytes 819216 | tf_op jit(solution)/shard_map/reduce_scatter | solution.py:17
  110.8 7.6 %all-to-all-start = ((bf16[192,16,1,80]{0,3,2,1:T(8,128)(2,1)}), bf16[192,16,1,80]{0,3,2,1:T(8,128)(2,1)S(1)}, u32[]{:S(2)}, u32[]{:S(2)}) async-start(bf16[192,16,1,80]{0,3,2,1:T(8,128)(2,1)} %bitcast.1), calls=%async_computation | async-start | bytes 1310720 | tf_op jit(solution)/shard_map/all_to_all | solution.py:107
  120.5 18.7 %all-to-all-done = bf16[192,16,1,80]{0,3,2,1:T(8,128)(2,1)S(1)} async-done(((bf16[192,16,1,80]{0,3,2,1:T(8,128)(2,1)}), bf16[192,16,1,80]{0,3,2,1:T(8,128)(2,1)S(1)}, u32[]{:S(2)}, u32[]{:S(2)}) %all-to-all-start) | async-done | bytes 491552 | tf_op jit(solution)/shard_map/all_to_all | solution.py:107
  139.3 4.9 %all-to-all-start.1 = ((bf16[192,16,1,80]{0,3,2,1:T(8,128)(2,1)}), bf16[192,16,1,80]{0,3,2,1:T(8,128)(2,1)S(1)}, u32[]{:S(2)}, u32[]{:S(2)}) async-start(bf16[192,16,1,80]{0,3,2,1:T(8,128)(2,1)} %bitcast.188), calls=%async_computation.1 | async-start | bytes 1310720 | tf_op jit(solution)/shard_map/all_to_all | solution.py:108
  144.1 3.2 convolution_convert_fusion.1
  149.9 7.1 %all-to-all-done.1 = bf16[192,16,1,80]{0,3,2,1:T(8,128)(2,1)S(1)} async-done(((bf16[192,16,1,80]{0,3,2,1:T(8,128)(2,1)}), bf16[192,16,1,80]{0,3,2,1:T(8,128)(2,1)S(1)}, u32[]{:S(2)}, u32[]{:S(2)}) %all-to-all-start.1) | async-done | bytes 491552 | tf_op jit(solution)/shard_map/all_to_all | solution.py:108
  157.0 11.4 %all_to_all.110 = f32[192,16,1]{0,2,1:T(1,128)S(1)} all-to-all(f32[192,16,1]{0,2,1:T(1,128)S(1)} %reduce_sum.30), channel_id=1, replica_groups=mesh['seq'=16,'dp_0'=2,'dp_1'=8] {'seq'}, dimensions={1} | all-to-all | bytes 24576 | tf_op jit(solution)/shard_map/all_to_all | solution.py:105
  168.4 4.4 %all-to-all-start.2 = ((bf16[192,16,1,80]{0,3,2,1:T(8,128)(2,1)}), bf16[192,16,1,80]{0,3,2,1:T(8,128)(2,1)}, u32[]{:S(2)}, u32[]{:S(2)}) async-start(bf16[192,16,1,80]{0,3,2,1:T(8,128)(2,1)} %bitcast.12), calls=%async_computation.2 | async-start | bytes 1310720 | tf_op jit(solution)/shard_map/all_to_all | solution.py:110
  174.3 2.4 copy.117
  178.2 7.7 %all-to-all-done.2 = bf16[192,16,1,80]{0,3,2,1:T(8,128)(2,1)} async-done(((bf16[192,16,1,80]{0,3,2,1:T(8,128)(2,1)}), bf16[192,16,1,80]{0,3,2,1:T(8,128)(2,1)}, u32[]{:S(2)}, u32[]{:S(2)}) %all-to-all-start.2) | async-done | bytes 491552 | tf_op jit(solution)/shard_map/all_to_all | solution.py:110
  186.0 2.3 copy.119
  188.3 100.8 %while.15 = (s32[]{:T(128)}, f32[3072,80]{0,1:T(8,128)S(1)}, f32[3072,80]{0,1:T(8,128)S(1)}, bf16[6,512,80]{1,2,0:T(8,128)(2,1)}, bf16[6,512,80]{2,1,0:T(8,128)(...) while((s32[]{:T(128)}, f32[3072,80]{0,1:T(8,128)S(1)}, ...), condition=%wide.region_4.5_spmd.clone, body=%wide.region_1.4_spmd.clone.sunk | while | flops 1281334784 | bytes 92938952 | solution.py:76
  188.3 2.0 multiply_reduce_fusion.2
  190.3 2.6 copy-done.1
  194.1 4.5 %convolution_add_fusion.5 = f32[3072,80]{0,1:T(8,128)S(1)} fusion(f32[512,3072]{1,0:T(8,128)} %copy-done.1, f32[512]{0:T(512)S(1)} %log_add_fusion.2, f32[3072,80]{0,1:T(8,128)S(1)} %get-tuple-element.223, pred[]{:T(512)S(6)} %compare.3, bf16[6,512,80]{2,1,0:T(8,128)(2,1)} %get-tuple-element.238, s32[]{:T(128)} %get-tuple-element.221), kind=kOutput, calls=%fused_computation.5.clone.1 | convolution fusion | flops 256868352 | bytes 8391169 | tf_op jit(solution)/shard_map/while/body/eval_jaxpr/dot_general | solution.py:57
  199.0 2.7 multiply_convert_fusion.2
  201.7 1.7 convolution_add_fusion.4
  203.4 1.7 fusion.65
  205.2 2.0 multiply_reduce_fusion.2
  207.1 2.6 copy-done.1
  210.9 4.3 %convolution_add_fusion.5 = f32[3072,80]{0,1:T(8,128)S(1)} fusion(f32[512,3072]{1,0:T(8,128)} %copy-done.1, f32[512]{0:T(512)S(1)} %log_add_fusion.2, f32[3072,80]{0,1:T(8,128)S(1)} %get-tuple-element.223, pred[]{:T(512)S(6)} %compare.3, bf16[6,512,80]{2,1,0:T(8,128)(2,1)} %get-tuple-element.238, s32[]{:T(128)} %get-tuple-element.221), kind=kOutput, calls=%fused_computation.5.clone.1 | convolution fusion | flops 256868352 | bytes 8391169 | tf_op jit(solution)/shard_map/while/body/eval_jaxpr/dot_general | solution.py:57
  215.7 2.7 multiply_convert_fusion.2
  218.4 1.7 convolution_add_fusion.4
  220.1 1.7 fusion.65
  221.9 2.0 multiply_reduce_fusion.2
  223.8 2.6 copy-done.1
  227.6 4.4 %convolution_add_fusion.5 = f32[3072,80]{0,1:T(8,128)S(1)} fusion(f32[512,3072]{1,0:T(8,128)} %copy-done.1, f32[512]{0:T(512)S(1)} %log_add_fusion.2, f32[3072,80]{0,1:T(8,128)S(1)} %get-tuple-element.223, pred[]{:T(512)S(6)} %compare.3, bf16[6,512,80]{2,1,0:T(8,128)(2,1)} %get-tuple-element.238, s32[]{:T(128)} %get-tuple-element.221), kind=kOutput, calls=%fused_computation.5.clone.1 | convolution fusion | flops 256868352 | bytes 8391169 | tf_op jit(solution)/shard_map/while/body/eval_jaxpr/dot_general | solution.py:57
  232.5 2.7 multiply_convert_fusion.2
  235.2 1.7 convolution_add_fusion.4
  236.9 1.7 fusion.65
  238.6 2.0 multiply_reduce_fusion.2
  240.6 2.6 copy-done.1
  244.4 4.4 %convolution_add_fusion.5 = f32[3072,80]{0,1:T(8,128)S(1)} fusion(f32[512,3072]{1,0:T(8,128)} %copy-done.1, f32[512]{0:T(512)S(1)} %log_add_fusion.2, f32[3072,80]{0,1:T(8,128)S(1)} %get-tuple-element.223, pred[]{:T(512)S(6)} %compare.3, bf16[6,512,80]{2,1,0:T(8,128)(2,1)} %get-tuple-element.238, s32[]{:T(128)} %get-tuple-element.221), kind=kOutput, calls=%fused_computation.5.clone.1 | convolution fusion | flops 256868352 | bytes 8391169 | tf_op jit(solution)/shard_map/while/body/eval_jaxpr/dot_general | solution.py:57
  249.5 2.7 multiply_convert_fusion.2
  252.2 1.7 convolution_add_fusion.4
  254.0 1.7 fusion.65
  255.7 2.0 multiply_reduce_fusion.2
  257.7 2.6 copy-done.1
  261.5 4.3 %convolution_add_fusion.5 = f32[3072,80]{0,1:T(8,128)S(1)} fusion(f32[512,3072]{1,0:T(8,128)} %copy-done.1, f32[512]{0:T(512)S(1)} %log_add_fusion.2, f32[3072,80]{0,1:T(8,128)S(1)} %get-tuple-element.223, pred[]{:T(512)S(6)} %compare.3, bf16[6,512,80]{2,1,0:T(8,128)(2,1)} %get-tuple-element.238, s32[]{:T(128)} %get-tuple-element.221), kind=kOutput, calls=%fused_computation.5.clone.1 | convolution fusion | flops 256868352 | bytes 8391169 | tf_op jit(solution)/shard_map/while/body/eval_jaxpr/dot_general | solution.py:57
  266.3 2.7 multiply_convert_fusion.2
  268.9 1.7 convolution_add_fusion.4
  270.7 1.7 fusion.65
  272.4 2.0 multiply_reduce_fusion.2
  274.4 2.6 copy-done.1
  278.2 4.3 %convolution_add_fusion.5 = f32[3072,80]{0,1:T(8,128)S(1)} fusion(f32[512,3072]{1,0:T(8,128)} %copy-done.1, f32[512]{0:T(512)S(1)} %log_add_fusion.2, f32[3072,80]{0,1:T(8,128)S(1)} %get-tuple-element.223, pred[]{:T(512)S(6)} %compare.3, bf16[6,512,80]{2,1,0:T(8,128)(2,1)} %get-tuple-element.238, s32[]{:T(128)} %get-tuple-element.221), kind=kOutput, calls=%fused_computation.5.clone.1 | convolution fusion | flops 256868352 | bytes 8391169 | tf_op jit(solution)/shard_map/while/body/eval_jaxpr/dot_general | solution.py:57
  283.0 2.7 multiply_convert_fusion.2
  285.6 1.7 convolution_add_fusion.4
  287.4 1.7 fusion.65
  289.1 2.2 copy.106
  303.5 4.1 %all-to-all-start.5 = ((bf16[16,192,1,1,80]{1,4,3,2,0:T(8,128)(2,1)}), bf16[16,192,1,1,80]{1,4,3,2,0:T(8,128)(2,1)S(1)}, u32[]{:S(2)}, u32[]{:S(2)}) async-start(bf16[16,192,1,1,80]{1,4,3,2,0:T(8,128)(2,1)} %fusion.24), calls=%async_computation.5 | async-start | bytes 1310720 | tf_op jit(solution)/shard_map/all_to_all | solution.py:127
  309.2 2.0 reduce.3
  311.5 2.2 reshape.100
  313.8 6.9 %all-to-all-done.5 = bf16[16,192,1,1,80]{1,4,3,2,0:T(8,128)(2,1)S(1)} async-done(((bf16[16,192,1,1,80]{1,4,3,2,0:T(8,128)(2,1)}), bf16[16,192,1,1,80]{1,4,3,2,0:T(8,128)(2,1)S(1)}, u32[]{:S(2)}, u32[]{:S(2)}) %all-to-all-start.5) | async-done | bytes 491552 | tf_op jit(solution)/shard_map/all_to_all | solution.py:127
  320.7 4.3 %all-to-all-start.6 = ((bf16[16,2,7680]{2,1,0:T(2,128)(2,1)}), bf16[16,2,7680]{2,1,0:T(2,128)(2,1)S(1)}, u32[]{:S(2)}, u32[]{:S(2)}) async-start(bf16[16,2,7680]{2,1,0:T(2,128)(2,1)} %reshape.100), calls=%async_computation.6 | async-start | bytes 983040 | tf_op jit(solution)/shard_map/all_to_all | solution.py:132
  324.9 2.0 reduce.4
  327.3 2.3 reshape.102
  329.5 6.5 %all-to-all-done.6 = bf16[16,2,7680]{2,1,0:T(2,128)(2,1)S(1)} async-done(((bf16[16,2,7680]{2,1,0:T(2,128)(2,1)}), bf16[16,2,7680]{2,1,0:T(2,128)(2,1)S(1)}, u32[]{:S(2)}, u32[]{:S(2)}) %all-to-all-start.6) | async-done | bytes 491552 | tf_op jit(solution)/shard_map/all_to_all | solution.py:132
  336.1 5.0 %all-to-all-start.7 = ((bf16[16,2,7680]{2,1,0:T(2,128)(2,1)}), bf16[16,2,7680]{2,1,0:T(2,128)(2,1)}, u32[]{:S(2)}, u32[]{:S(2)}) async-start(bf16[16,2,7680]{2,1,0:T(2,128)(2,1)} %reshape.102), calls=%async_computation.7 | async-start | bytes 983040 | tf_op jit(solution)/shard_map/all_to_all | solution.py:133
  342.1 5.3 %reshape.101 = bf16[3072,1,1,80]{3,2,1,0:T(2,128)(2,1)S(1)} reshape(bf16[16,2,7680]{2,1,0:T(2,128)(2,1)} %copy-done.7) | data formatting | bytes 983040
  352.3 5.3 %reshape.103 = bf16[3072,1,1,80]{3,2,1,0:T(2,128)(2,1)S(1)} reshape(bf16[16,2,7680]{2,1,0:T(2,128)(2,1)} %all-to-all-done.7) | data formatting | bytes 983040
  361.1 4.0 %reduce_sum.31 = f32[80,1280]{1,0:T(8,128)} reduce(f32[16,80,1280]{2,1,0:T(8,128)} %all-gather.5.cloned.1.call-done, f32[]{:T(128)} %constant.13.clone.1), dimensions={0}, to_apply=%region_7.8 | reduce | flops 1536000 | bytes 6963204 | tf_op jit(solution)/shard_map/reduce_sum | solution.py:33
  (121 shorter events, 46.1 us)
Async XLA Ops:
  8.0 1.0 copy-start
  8.0 101.6 %reduce-scatter.3.cloned.1.call-start = ((), (), s32[]{:S(2)}) async-start(), calls=%async_computation.11 | async-start | bytes 7372800 | tf_op jit(solution)/shard_map/reduce_scatter | solution.py:17
  14.3 1.0 copy-start.8
  14.3 95.3 %copy-start.9 = (bf16[1,192,1280]{2,1,0:T(8,128)(2,1)S(1)}, bf16[1,192,1280]{2,1,0:T(8,128)(2,1)}, u32[]{:S(2)}) copy-start(bf16[1,192,1280]{2,1,0:T(8,128)(2,1)} %param.8) | copy-start | bytes 1474564
  14.3 104.0 %copy-start.4 = (bf16[1,192,1280]{2,1,0:T(8,128)(2,1)S(1)}, bf16[1,192,1280]{2,1,0:T(8,128)(2,1)}, u32[]{:S(2)}) copy-start(bf16[1,192,1280]{2,1,0:T(8,128)(2,1)} %param.11) | copy-start | bytes 1474564
  14.3 105.1 %copy-start.10 = (bf16[1,192,1280]{2,1,0:T(8,128)(2,1)S(1)}, bf16[1,192,1280]{2,1,0:T(8,128)(2,1)}, u32[]{:S(2)}) copy-start(bf16[1,192,1280]{2,1,0:T(8,128)(2,1)} %param.9) | copy-start | bytes 1474564
  14.4 129.8 %all-gather.3.cloned.1.call-start = ((), (), s32[]{:S(2)}) async-start(), calls=%async_computation.10 | async-start | bytes 3481600 | tf_op jit(solution)/shard_map/all_gather | solution.py:94
  16.4 94.3 %all-to-all-start.3 = ((bf16[192,16,1,80]{0,3,2,1:T(8,128)(2,1)}), bf16[192,16,1,80]{0,3,2,1:T(8,128)(2,1)S(1)}, u32[]{:S(2)}, u32[]{:S(2)}) async-start(bf16[192,16,1,80]{0,3,2,1:T(8,128)(2,1)} %bitcast.17), calls=%async_computation.3 | async-start | bytes 1310720 | tf_op jit(solution)/shard_map/all_to_all | solution.py:109
  24.9 163.3 %reduce-scatter.5.cloned.1.call-start = ((), (), s32[]{:S(2)}) async-start(), calls=%async_computation.12 | async-start | bytes 1228800 | tf_op jit(solution)/shard_map/reduce_scatter | solution.py:17
  110.8 28.5 %all-to-all-start = ((bf16[192,16,1,80]{0,3,2,1:T(8,128)(2,1)}), bf16[192,16,1,80]{0,3,2,1:T(8,128)(2,1)S(1)}, u32[]{:S(2)}, u32[]{:S(2)}) async-start(bf16[192,16,1,80]{0,3,2,1:T(8,128)(2,1)} %bitcast.1), calls=%async_computation | async-start | bytes 1310720 | tf_op jit(solution)/shard_map/all_to_all | solution.py:107
  139.3 33.5 %copy-start.5 = (bf16[192,16,1,80]{0,3,2,1:T(8,128)(2,1)}, bf16[192,16,1,80]{0,3,2,1:T(8,128)(2,1)S(1)}, u32[]{:S(2)}) copy-start(bf16[192,16,1,80]{0,3,2,1:T(8,128)(2,1)S(1)} %all-to-all-done) | copy-start | bytes 1474564
  139.3 17.8 %all-to-all-start.1 = ((bf16[192,16,1,80]{0,3,2,1:T(8,128)(2,1)}), bf16[192,16,1,80]{0,3,2,1:T(8,128)(2,1)S(1)}, u32[]{:S(2)}, u32[]{:S(2)}) async-start(bf16[192,16,1,80]{0,3,2,1:T(8,128)(2,1)} %bitcast.188), calls=%async_computation.1 | async-start | bytes 1310720 | tf_op jit(solution)/shard_map/all_to_all | solution.py:108
  157.0 16.0 %copy-start.6 = (bf16[192,16,1,80]{0,3,2,1:T(8,128)(2,1)}, bf16[192,16,1,80]{0,3,2,1:T(8,128)(2,1)S(1)}, u32[]{:S(2)}) copy-start(bf16[192,16,1,80]{0,3,2,1:T(8,128)(2,1)S(1)} %all-to-all-done.1) | copy-start | bytes 1474564
  168.4 17.5 %all-to-all-start.2 = ((bf16[192,16,1,80]{0,3,2,1:T(8,128)(2,1)}), bf16[192,16,1,80]{0,3,2,1:T(8,128)(2,1)}, u32[]{:S(2)}, u32[]{:S(2)}) async-start(bf16[192,16,1,80]{0,3,2,1:T(8,128)(2,1)} %bitcast.12), calls=%async_computation.2 | async-start | bytes 1310720 | tf_op jit(solution)/shard_map/all_to_all | solution.py:110
  172.8 188.3 %all-gather.5.cloned.1.call-start = ((), (), s32[]{:S(2)}) async-start(), calls=%async_computation.13 | async-start | bytes 6963200 | tf_op jit(solution)/shard_map/all_gather | solution.py:32
  190.2 2.6 copy-start.1
  194.0 4.8 %copy-start.2 = (f32[512,3072]{1,0:T(8,128)S(1)}, f32[512,3072]{1,0:T(8,128)}, u32[]{:S(2)}) copy-start(f32[512,3072]{1,0:T(8,128)} %copy-done.1) | copy-start | bytes 18874372 | tf_op jit(solution)/shard_map/while
  194.0 5.0 %copy-start.3 = (bf16[3072,80]{1,0:T(8,128)(2,1)S(1)}, bf16[3072,80]{1,0:T(8,128)(2,1)}, u32[]{:S(2)}) copy-start(bf16[3072,80]{1,0:T(8,128)(2,1)} %get-tuple-element.239) | copy-start | bytes 1474564 | tf_op jit(solution)/shard_map/while
  207.1 2.6 copy-start.1
  210.9 4.6 %copy-start.2 = (f32[512,3072]{1,0:T(8,128)S(1)}, f32[512,3072]{1,0:T(8,128)}, u32[]{:S(2)}) copy-start(f32[512,3072]{1,0:T(8,128)} %copy-done.1) | copy-start | bytes 18874372 | tf_op jit(solution)/shard_map/while
  210.9 4.8 %copy-start.3 = (bf16[3072,80]{1,0:T(8,128)(2,1)S(1)}, bf16[3072,80]{1,0:T(8,128)(2,1)}, u32[]{:S(2)}) copy-start(bf16[3072,80]{1,0:T(8,128)(2,1)} %get-tuple-element.239) | copy-start | bytes 1474564 | tf_op jit(solution)/shard_map/while
  223.8 2.6 copy-start.1
  227.6 4.7 %copy-start.2 = (f32[512,3072]{1,0:T(8,128)S(1)}, f32[512,3072]{1,0:T(8,128)}, u32[]{:S(2)}) copy-start(f32[512,3072]{1,0:T(8,128)} %copy-done.1) | copy-start | bytes 18874372 | tf_op jit(solution)/shard_map/while
  227.6 4.9 %copy-start.3 = (bf16[3072,80]{1,0:T(8,128)(2,1)S(1)}, bf16[3072,80]{1,0:T(8,128)(2,1)}, u32[]{:S(2)}) copy-start(bf16[3072,80]{1,0:T(8,128)(2,1)} %get-tuple-element.239) | copy-start | bytes 1474564 | tf_op jit(solution)/shard_map/while
  240.6 2.6 copy-start.1
  244.4 4.9 %copy-start.2 = (f32[512,3072]{1,0:T(8,128)S(1)}, f32[512,3072]{1,0:T(8,128)}, u32[]{:S(2)}) copy-start(f32[512,3072]{1,0:T(8,128)} %copy-done.1) | copy-start | bytes 18874372 | tf_op jit(solution)/shard_map/while
  244.4 5.1 %copy-start.3 = (bf16[3072,80]{1,0:T(8,128)(2,1)S(1)}, bf16[3072,80]{1,0:T(8,128)(2,1)}, u32[]{:S(2)}) copy-start(bf16[3072,80]{1,0:T(8,128)(2,1)} %get-tuple-element.239) | copy-start | bytes 1474564 | tf_op jit(solution)/shard_map/while
  257.7 2.6 copy-start.1
  261.5 4.6 %copy-start.2 = (f32[512,3072]{1,0:T(8,128)S(1)}, f32[512,3072]{1,0:T(8,128)}, u32[]{:S(2)}) copy-start(f32[512,3072]{1,0:T(8,128)} %copy-done.1) | copy-start | bytes 18874372 | tf_op jit(solution)/shard_map/while
  261.5 4.8 %copy-start.3 = (bf16[3072,80]{1,0:T(8,128)(2,1)S(1)}, bf16[3072,80]{1,0:T(8,128)(2,1)}, u32[]{:S(2)}) copy-start(bf16[3072,80]{1,0:T(8,128)(2,1)} %get-tuple-element.239) | copy-start | bytes 1474564 | tf_op jit(solution)/shard_map/while
  274.4 2.6 copy-start.1
  278.2 4.6 %copy-start.2 = (f32[512,3072]{1,0:T(8,128)S(1)}, f32[512,3072]{1,0:T(8,128)}, u32[]{:S(2)}) copy-start(f32[512,3072]{1,0:T(8,128)} %copy-done.1) | copy-start | bytes 18874372 | tf_op jit(solution)/shard_map/while
  278.2 4.8 %copy-start.3 = (bf16[3072,80]{1,0:T(8,128)(2,1)S(1)}, bf16[3072,80]{1,0:T(8,128)(2,1)}, u32[]{:S(2)}) copy-start(bf16[3072,80]{1,0:T(8,128)(2,1)} %get-tuple-element.239) | copy-start | bytes 1474564 | tf_op jit(solution)/shard_map/while
  303.5 17.2 %all-to-all-start.5 = ((bf16[16,192,1,1,80]{1,4,3,2,0:T(8,128)(2,1)}), bf16[16,192,1,1,80]{1,4,3,2,0:T(8,128)(2,1)S(1)}, u32[]{:S(2)}, u32[]{:S(2)}) async-start(bf16[16,192,1,1,80]{1,4,3,2,0:T(8,128)(2,1)} %fusion.24), calls=%async_computation.5 | async-start | bytes 1310720 | tf_op jit(solution)/shard_map/all_to_all | solution.py:127
  320.7 15.4 %all-to-all-start.6 = ((bf16[16,2,7680]{2,1,0:T(2,128)(2,1)}), bf16[16,2,7680]{2,1,0:T(2,128)(2,1)S(1)}, u32[]{:S(2)}, u32[]{:S(2)}) async-start(bf16[16,2,7680]{2,1,0:T(2,128)(2,1)} %reshape.100), calls=%async_computation.6 | async-start | bytes 983040 | tf_op jit(solution)/shard_map/all_to_all | solution.py:132
  336.1 5.0 %copy-start.7 = (bf16[16,2,7680]{2,1,0:T(2,128)(2,1)}, bf16[16,2,7680]{2,1,0:T(2,128)(2,1)S(1)}, u32[]{:S(2)}) copy-start(bf16[16,2,7680]{2,1,0:T(2,128)(2,1)S(1)} %all-to-all-done.6) | copy-start | bytes 1474564
  336.1 16.3 %all-to-all-start.7 = ((bf16[16,2,7680]{2,1,0:T(2,128)(2,1)}), bf16[16,2,7680]{2,1,0:T(2,128)(2,1)}, u32[]{:S(2)}, u32[]{:S(2)}) async-start(bf16[16,2,7680]{2,1,0:T(2,128)(2,1)} %reshape.102), calls=%async_computation.7 | async-start | bytes 983040 | tf_op jit(solution)/shard_map/all_to_all | solution.py:133
Sparse Core Ops, SparseCore 0:
  14.5 95.1 reduce-scatter.2
  112.2 40.2 reduce-scatter.4
  188.4 64.0 all-gather.4
Sparse Core Ops, SparseCore 1:
  16.6 123.6 all-gather.2
